TPU v7x, 32 devices: a whole 2x2x4 slice. The times are simulated.
32 devices in a mesh: seq: 16 (over z, y, core), dp: 2 (over x).
Axes of the slice: x: 2, y: 2, z: 4, core: 2. Of those that a mesh axis runs over, the one named last changes fastest.
Arguments:
- queries: bfloat16 [2, 2048, 1024], P('dp', 'seq'), may hold values from -6 to 6
- keys: bfloat16 [2, 2048, 1024], P('dp', 'seq'), may hold values from -6 to 6
- values: bfloat16 [2, 2048, 1024], P('dp', 'seq'), may hold values from -6 to 6
- d_out: bfloat16 [2, 2048, 1024], P('dp', 'seq'), may hold values from -6 to 6
- segment_ids: int32 [2, 2048], P('dp', 'seq'), may hold values from 0 to 2, never falling along the last dimension, each value on 1 to 1536 neighbouring positions
- block_bucket: int32 [2, 16], P('dp', 'seq'), may hold values from 0 to 63
- block_mask: int32 [2, 16, 5, 1], P('dp', 'seq'), may hold values 0 or 1
- bias_table: bfloat16 [16, 64, 64], replicated, may hold values from -4 to 4
Outputs:
- attention_out: bfloat16 [2, 2048, 1024], P('dp', 'seq')
- d_queries: bfloat16 [2, 2048, 1024], P('dp', 'seq')
- d_keys: bfloat16 [2, 2048, 1024], P('dp', 'seq')
- d_values: bfloat16 [2, 2048, 1024], P('dp', 'seq')
- d_table: float32 [16, 64, 64], replicated
Inputs may be any that keep to these rules, and one draw needn't show every extreme that they name: `segment_ids`: each document is a run of consecutive tokens of one sequence.
All inputs are finite; a program needn't handle non-finite values. No bound on the sum of `block_mask` on one device may be relied on, other than what follows from the above.
Results may differ from a plain program's by a relative error of at most 0.024.
Values may be sent and summed in bfloat16 or wider, within the bound.
No kernel may reach another device: no remote copies, remote signals or barrier semaphores. Data moves between devices by JAX's collectives and lax.ppermute only.
A program may use at most 64 MiB of HBM per device.

v0:
```python
import jax
import jax.numpy as jnp
from jax import lax
from jax.sharding import PartitionSpec as P

H = 16
DH = 64
NB = 64
BLK = 128
masked_value = -1e30


def from_partner(value, axis, apart):
    mask = 2**apart
    pairs = [(source, source ^ mask) for source in range(lax.axis_size(axis))]
    return lax.ppermute(value, axis, pairs)


def expand_blocks(bias_block, row_count, col_count):
    leading = bias_block.shape[:-2]
    row_blocks = bias_block.shape[-2]
    col_blocks = bias_block.shape[-1]
    widened = jnp.broadcast_to(
        bias_block[..., :, None, :, None],
        leading + (row_blocks, row_count // row_blocks, col_blocks, col_count // col_blocks),
    )
    return widened.reshape(leading + (row_count, col_count))


def one_hot_rows(buckets):
    levels_all = jnp.arange(NB, dtype=jnp.float32)
    return (buckets.astype(jnp.float32)[:, None] == levels_all[None, :]).astype(jnp.bfloat16)


def bias_tile(bias_table, row_hot, col_hot):
    picked = jnp.einsum(
        "bn,hnm->hbm", row_hot, bias_table, preferred_element_type=jnp.float32
    ).astype(jnp.bfloat16)
    return jnp.einsum("hbm,cm->hbc", picked, col_hot, preferred_element_type=jnp.float32)


def allowed_pairs(seg_rows, seg_cols, block_ok):
    same_doc = seg_rows.astype(jnp.float32)[:, None] == seg_cols.astype(jnp.float32)[None, :]
    return same_doc & expand_blocks(block_ok, seg_rows.shape[0], seg_cols.shape[0])


def masked_scores(query_heads, key_heads, bias_block, allowed):
    products = jnp.einsum(
        "thd,uhd->htu", query_heads, key_heads, preferred_element_type=jnp.float32
    )
    shifted = products * 0.125 + expand_blocks(bias_block, query_heads.shape[0], key_heads.shape[0])
    return jnp.where(allowed[None], shifted, masked_value)


def grad_terms(scores, allowed, lse, row_delta, grad_heads, value_heads):
    probs = jnp.where(allowed[None], jnp.exp(scores - lse[:, :, None]), 0.0)
    dprob = jnp.einsum("thd,uhd->htu", grad_heads, value_heads, preferred_element_type=jnp.float32)
    dscore = probs * (dprob - row_delta[:, :, None])
    return (probs.astype(jnp.bfloat16), dscore)


def local(queries, keys, values, d_out, segment_ids, block_bucket, block_mask, bias_table):
    row_count = queries.shape[1]
    block_count = row_count // BLK
    level_count = lax.axis_size("seq").bit_length() - 1
    query_heads = queries[0].reshape(row_count, H, DH)
    grad_heads = d_out[0].reshape(row_count, H, DH)
    own_keys = keys[0]
    own_values = values[0]
    own_seg = segment_ids[0]
    own_bucket = block_bucket[0]
    own_mask = block_mask[0] != 0
    own_hot = one_hot_rows(own_bucket)
    own_hot_wide = own_hot.astype(jnp.float32)
    section_list = list(range(level_count + 1))
    stored = {}
    run_max = jnp.full((H, row_count), masked_value, jnp.float32)
    run_sum = jnp.zeros((H, row_count), jnp.float32)
    run_acc = jnp.zeros((row_count, H, DH), jnp.float32)
    for section_num in section_list:
        if section_num == 0:
            key_rows, value_rows, seg_cols, bucket_cols = (
                own_keys,
                own_values,
                own_seg,
                own_bucket,
            )
            block_ok = own_mask[:, 0, :] | jnp.eye(block_count, dtype=bool)
        else:
            key_rows, value_rows, seg_cols, bucket_cols = from_partner(
                (
                    own_keys,
                    own_values,
                    own_seg.astype(jnp.bfloat16),
                    own_bucket.astype(jnp.bfloat16),
                ),
                "seq",
                section_num - 1,
            )
            block_ok = own_mask[:, section_num, :]
        key_heads = key_rows.reshape(row_count, H, DH)
        value_heads = value_rows.reshape(row_count, H, DH)
        col_hot = one_hot_rows(bucket_cols)
        bias_block = bias_tile(bias_table, own_hot, col_hot)
        allowed = allowed_pairs(own_seg, seg_cols, block_ok)
        stored[section_num] = (key_heads, value_heads, seg_cols, col_hot, bias_block, allowed)
        scores = masked_scores(query_heads, key_heads, bias_block, allowed)
        fresh_max = jnp.maximum(run_max, jnp.max(scores, axis=-1))
        rescale = jnp.exp(run_max - fresh_max)
        weights = jnp.where(allowed[None], jnp.exp(scores - fresh_max[:, :, None]), 0.0)
        run_sum = run_sum * rescale + jnp.sum(weights, axis=-1)
        run_acc = run_acc * rescale.T[:, :, None] + jnp.einsum(
            "htu,uhd->thd",
            weights.astype(jnp.bfloat16),
            value_heads,
            preferred_element_type=jnp.float32,
        )
        run_max = fresh_max
    out_heads = (run_acc / run_sum.T[:, :, None]).astype(jnp.bfloat16)
    lse = run_max + jnp.log(run_sum)
    row_delta = jnp.sum(out_heads.astype(jnp.float32) * grad_heads.astype(jnp.float32), axis=-1).T
    out_rows = out_heads.reshape(row_count, H * DH)
    query_acc = jnp.zeros((row_count, H, DH), jnp.float32)
    key_acc = jnp.zeros((row_count, H, DH), jnp.float32)
    value_acc = jnp.zeros((row_count, H, DH), jnp.float32)
    table_acc = jnp.zeros((H, NB, NB), jnp.float32)
    for section_num in section_list:
        key_heads, value_heads, seg_cols, col_hot, bias_block, allowed = stored[section_num]
        scores = masked_scores(query_heads, key_heads, bias_block, allowed)
        probs_low, dscore = grad_terms(scores, allowed, lse, row_delta, grad_heads, value_heads)
        dscore_low = dscore.astype(jnp.bfloat16)
        query_acc = (
            query_acc
            + jnp.einsum("htu,uhd->thd", dscore_low, key_heads, preferred_element_type=jnp.float32)
            * 0.125
        )
        block_sums = dscore.reshape(H, block_count, BLK, block_count, BLK).sum(axis=(2, 4))
        table_acc = table_acc + jnp.einsum(
            "bn,hbc,cm->hnm",
            own_hot_wide,
            block_sums,
            col_hot.astype(jnp.float32),
            precision=lax.Precision.HIGHEST,
        )
        if section_num == 0:
            key_acc = (
                jnp.einsum(
                    "htu,thd->uhd", dscore_low, query_heads, preferred_element_type=jnp.float32
                )
                * 0.125
            )
            value_acc = jnp.einsum(
                "htu,thd->uhd", probs_low, grad_heads, preferred_element_type=jnp.float32
            )
        else:
            key_term = (
                jnp.einsum(
                    "htu,thd->uhd", dscore_low, query_heads, preferred_element_type=jnp.float32
                )
                * 0.125
            ).astype(jnp.bfloat16)
            value_term = jnp.einsum(
                "htu,thd->uhd", probs_low, grad_heads, preferred_element_type=jnp.float32
            ).astype(jnp.bfloat16)
            back_keys, back_values = from_partner(
                (key_term.reshape(row_count, H * DH), value_term.reshape(row_count, H * DH)),
                "seq",
                section_num - 1,
            )
            key_acc = key_acc + back_keys.reshape(row_count, H, DH).astype(jnp.float32)
            value_acc = value_acc + back_values.reshape(row_count, H, DH).astype(jnp.float32)
    table_total = lax.psum(table_acc, ("seq", "dp"))
    feature_count = H * DH
    return (
        out_rows.reshape(1, row_count, feature_count),
        query_acc.astype(jnp.bfloat16).reshape(1, row_count, feature_count),
        key_acc.astype(jnp.bfloat16).reshape(1, row_count, feature_count),
        value_acc.astype(jnp.bfloat16).reshape(1, row_count, feature_count),
        table_total,
    )


def solution(mesh):
    in_specs = (
        P("dp", "seq", None),
        P("dp", "seq", None),
        P("dp", "seq", None),
        P("dp", "seq", None),
        P("dp", "seq"),
        P("dp", "seq"),
        P("dp", "seq", None, None),
        P(),
    )
    out_specs = (
        P("dp", "seq", None),
        P("dp", "seq", None),
        P("dp", "seq", None),
        P("dp", "seq", None),
        P(),
    )
    return jax.shard_map(local, mesh=mesh, in_specs=in_specs, out_specs=out_specs, check_vma=False)
```

profile of v0, /device:TPU:0, one launch (start us, length us, event | category | flops | bytes accessed | tf_op | source)
XLA Modules:
  0.0 256.8 jit_solution(7733567742736410515)
XLA Ops:
  8.0 3.0 %collective-permute-start.4 = (bf16[128]{0:T(256)(128)(2,1)S(1)}, bf16[128]{0:T(256)(128)(2,1)S(1)}, u32[]{:S(2)}, u32[]{:S(2)}) collective-permute-start(bf16[128]{0:T(256)(128)(2,1)S(1)} %get-tuple-element.40), channel_id=1, source_target_pairs={{0,4},{2,6},{4,0},{6,2},{8,12},{10,14},{12,8},{14,10},{16,20},{18,... | collective-permute-start | bytes 776 | tf_op jit(solution)/shard_map/ppermute | solution.py:16
  10.9 1.6 collective-permute-start.8
  12.5 2.6 %collective-permute-start.12 = (bf16[128]{0:T(256)(128)(2,1)S(1)}, bf16[128]{0:T(256)(128)(2,1)S(1)}, u32[]{:S(2)}, u32[]{:S(2)}) collective-permute-start(bf16[128]{0:T(256)(128)(2,1)S(1)} %get-tuple-element.40), channel_id=1, source_target_pairs={{0,16},{2,18},{4,20},{6,22},{8,24},{10,26},{12,28},{14,30},{16,0},... | collective-permute-start | bytes 776 | tf_op jit(solution)/shard_map/ppermute | solution.py:16
  15.8 1.7 collective-permute-start.14
  23.2 1.8 collective-permute-start.10
  26.7 1.8 collective-permute-start.6
  31.8 2.6 %collective-permute-start.13 = (bf16[128,1024]{1,0:T(8,128)(2,1)}, bf16[128,1024]{1,0:T(8,128)(2,1)S(1)}, u32[]{:S(2)}, u32[]{:S(2)}) collective-permute-start(bf16[128,1024]{1,0:T(8,128)(2,1)} %bitcast.15), channel_id=1, source_target_pairs={{0,16},{2,18},{4,20},{6,22},{8,24},{10,26},{12,28},{14,30},{16,0},... | collective-permute-start | bytes 786440 | tf_op jit(solution)/shard_map/ppermute | solution.py:16
  38.0 2.6 %broadcast_compare_fusion = (pred[128,128]{0,1:T(8,128)(4,1)S(1)}, pred[128,128]{0,1:T(8,128)(4,1)S(1)}, pred[128,128]{0,1:T(8,128)(4,1)S(1)}, pred[128,128]{0,1:T(8,128)(4,1)S(1)}, pred[128,128]{0,1:T(8,128)(4,1)S(1)}) fusion(f32[128]{0:T(128)S(1)} %get-tuple-element.41, pred[]{:T(512)} %bitcast.25, f32[128]{0:T(128)S(1)} %convert_element_type.245, ...), kind=kLoop, calls=%fused_computation.151 | loop fusion | flops 147456 | bytes 84484 | tf_op jit(solution)/shard_map/eq | solution.py:43
  41.1 6.8 %collective-permute-done.13 = bf16[128,1024]{1,0:T(8,128)(2,1)S(1)} collective-permute-done((bf16[128,1024]{1,0:T(8,128)(2,1)}, bf16[128,1024]{1,0:T(8,128)(2,1)S(1)}, u32[]{:S(2)}, u32[]{:S(2)}) %collective-permute-start.13) | collective-permute-done | bytes 262176 | tf_op jit(solution)/shard_map/ppermute | solution.py:16
  51.4 1.8 copy.75
  53.2 2.3 fusion.151
  55.5 1.8 copy.72
  57.3 2.3 fusion.152
  59.6 1.8 copy.69
  61.4 1.5 fusion.153
  66.0 1.8 copy.79
  67.8 2.0 convolution_bitcast_fusion
  69.9 1.8 copy.76
  71.7 2.4 convolution_bitcast_fusion.1
  74.1 1.8 copy.73
  75.8 2.4 convolution_bitcast_fusion.2
  78.3 1.8 copy.70
  80.8 3.1 %multiply_reduce_fusion = (f32[128,16]{0,1:T(8,128)S(1)}, bf16[128,16,64]{0,2,1:T(8,128)(2,1)}) fusion(bf16[128,16,64]{0,2,1:T(8,128)(2,1)S(1)} %bitcast.299, f32[128,16]{0,1:T(8,128)S(1)} %copy-done.24, f32[128,16,64]{0,2,1:T(8,128)} %convolution_bitcast_fusion, f32[128,16]{0,1:T(8,128)S(1)} %copy-done.27, f32[128,16,64]{0,2,1:T(8,128)} %convolution_bitcast_fusion.1, ...), kind=kOutput, calls=%fused_computation.103 | convolution fusion | flops 36042752 | bytes 3997696 | tf_op jit(solution)/shard_map/htu,uhd->thd/dot_general | solution.py:112
  99.8 1.9 copy.102
  106.1 1.9 copy.103
  108.0 2.9 %collective-permute-start.19 = (bf16[128,1024]{0,1:T(8,128)(2,1)}, bf16[128,1024]{0,1:T(8,128)(2,1)}, u32[]{:S(2)}, u32[]{:S(2)}) collective-permute-start(bf16[128,1024]{0,1:T(8,128)(2,1)} %bitcast.353), channel_id=1, source_target_pairs={{0,16},{2,18},{4,20},{6,22},{8,24},{10,26},{12,28},{14,30},{16,0},... | collective-permute-start | bytes 786440 | tf_op jit(solution)/shard_map/ppermute | solution.py:16
  111.7 2.0 collective-permute-start.23
  113.8 1.5 multiply_add_fusion
  115.9 8.2 %collective-permute-done.19 = bf16[128,1024]{0,1:T(8,128)(2,1)} collective-permute-done((bf16[128,1024]{0,1:T(8,128)(2,1)}, bf16[128,1024]{0,1:T(8,128)(2,1)}, u32[]{:S(2)}, u32[]{:S(2)}) %collective-permute-start.19) | collective-permute-done | bytes 262176 | tf_op jit(solution)/shard_map/ppermute | solution.py:16
  127.2 9.0 %collective-permute-done.23 = bf16[128,1024]{0,1:T(8,128)(2,1)S(1)} collective-permute-done((bf16[128,1024]{0,1:T(8,128)(2,1)}, bf16[128,1024]{0,1:T(8,128)(2,1)S(1)}, u32[]{:S(2)}, u32[]{:S(2)}) %collective-permute-start.23) | collective-permute-done | bytes 262176 | tf_op jit(solution)/shard_map/ppermute | solution.py:16
  139.2 108.9 %all-reduce.2.cloned.1.call-done = f32[16,64,64]{2,1,0:T(8,128)} async-done(((f32[16,64,64]{2,1,0:T(8,128)}), f32[16,64,64]{2,1,0:T(8,128)}) %all-reduce.2.cloned.1.call-update) | async-done | bytes 262160 | tf_op jit(solution)/shard_map/psum | solution.py:172
  248.1 1.9 copy.134
  (162 shorter events, 48.1 us)
Async XLA Ops:
  7.2 12.0 %copy-start = (bf16[16,64,64]{2,1,0:T(8,128)(2,1)S(1)}, bf16[16,64,64]{2,1,0:T(8,128)(2,1)}, u32[]{:S(2)}) copy-start(bf16[16,64,64]{2,1,0:T(8,128)(2,1)} %param.15) | copy-start | bytes 393220
  7.2 240.9 %all-reduce.2.cloned.1.call-start = ((), (), s32[]{:S(2)}) async-start(), calls=%async_computation | async-start | bytes 1048576 | tf_op jit(solution)/shard_map/psum | solution.py:172
  8.0 27.9 %collective-permute-start.4 = (bf16[128]{0:T(256)(128)(2,1)S(1)}, bf16[128]{0:T(256)(128)(2,1)S(1)}, u32[]{:S(2)}, u32[]{:S(2)}) collective-permute-start(bf16[128]{0:T(256)(128)(2,1)S(1)} %get-tuple-element.40), channel_id=1, source_target_pairs={{0,4},{2,6},{4,0},{6,2},{8,12},{10,14},{12,8},{14,10},{16,20},{18,... | collective-permute-start | bytes 776 | tf_op jit(solution)/shard_map/ppermute | solution.py:16
  10.9 25.5 %collective-permute-start.8 = (bf16[128]{0:T(256)(128)(2,1)S(1)}, bf16[128]{0:T(256)(128)(2,1)S(1)}, u32[]{:S(2)}, u32[]{:S(2)}) collective-permute-start(bf16[128]{0:T(256)(128)(2,1)S(1)} %get-tuple-element.40), channel_id=1, source_target_pairs={{0,8},{2,10},{4,12},{6,14},{8,0},{10,2},{12,4},{14,6},{16,24},{18,... | collective-permute-start | bytes 776 | tf_op jit(solution)/shard_map/ppermute | solution.py:16
  12.5 25.1 %collective-permute-start.12 = (bf16[128]{0:T(256)(128)(2,1)S(1)}, bf16[128]{0:T(256)(128)(2,1)S(1)}, u32[]{:S(2)}, u32[]{:S(2)}) collective-permute-start(bf16[128]{0:T(256)(128)(2,1)S(1)} %get-tuple-element.40), channel_id=1, source_target_pairs={{0,16},{2,18},{4,20},{6,22},{8,24},{10,26},{12,28},{14,30},{16,0},... | collective-permute-start | bytes 776 | tf_op jit(solution)/shard_map/ppermute | solution.py:16
  15.1 22.5 %collective-permute-start = (bf16[128]{0:T(256)(128)(2,1)S(1)}, bf16[128]{0:T(256)(128)(2,1)S(1)}, u32[]{:S(2)}, u32[]{:S(2)}) collective-permute-start(bf16[128]{0:T(256)(128)(2,1)S(1)} %get-tuple-element.40), channel_id=1, source_target_pairs={{0,2},{2,0},{4,6},{6,4},{8,10},{10,8},{12,14},{14,12},{16,18},{18,... | collective-permute-start | bytes 776 | tf_op jit(solution)/shard_map/ppermute | solution.py:16
  15.8 7.4 %collective-permute-start.14 = (bf16[1]{0:T(256)(128)(2,1)}, bf16[1]{0:T(256)(128)(2,1)}, u32[]{:S(2)}, u32[]{:S(2)}) collective-permute-start(bf16[1]{0:T(256)(128)(2,1)} %bitcast.17), channel_id=1, source_target_pairs={{0,16},{2,18},{4,20},{6,22},{8,24},{10,26},{12,28},{14,30},{16,0},... | collective-permute-start | bytes 14 | tf_op jit(solution)/shard_map/ppermute | solution.py:16
  23.2 3.6 %collective-permute-start.10 = (bf16[1]{0:T(256)(128)(2,1)}, bf16[1]{0:T(256)(128)(2,1)}, u32[]{:S(2)}, u32[]{:S(2)}) collective-permute-start(bf16[1]{0:T(256)(128)(2,1)} %bitcast.17), channel_id=1, source_target_pairs={{0,8},{2,10},{4,12},{6,14},{8,0},{10,2},{12,4},{14,6},{16,24},{18,... | collective-permute-start | bytes 14 | tf_op jit(solution)/shard_map/ppermute | solution.py:16
  26.7 3.5 %collective-permute-start.6 = (bf16[1]{0:T(256)(128)(2,1)}, bf16[1]{0:T(256)(128)(2,1)}, u32[]{:S(2)}, u32[]{:S(2)}) collective-permute-start(bf16[1]{0:T(256)(128)(2,1)} %bitcast.17), channel_id=1, source_target_pairs={{0,4},{2,6},{4,0},{6,2},{8,12},{10,14},{12,8},{14,10},{16,20},{18,... | collective-permute-start | bytes 14 | tf_op jit(solution)/shard_map/ppermute | solution.py:16
  30.2 1.6 collective-permute-start.2
  31.8 16.0 %collective-permute-start.13 = (bf16[128,1024]{1,0:T(8,128)(2,1)}, bf16[128,1024]{1,0:T(8,128)(2,1)S(1)}, u32[]{:S(2)}, u32[]{:S(2)}) collective-permute-start(bf16[128,1024]{1,0:T(8,128)(2,1)} %bitcast.15), channel_id=1, source_target_pairs={{0,16},{2,18},{4,20},{6,22},{8,24},{10,26},{12,28},{14,30},{16,0},... | collective-permute-start | bytes 786440 | tf_op jit(solution)/shard_map/ppermute | solution.py:16
  35.8 14.4 %collective-permute-start.9 = (bf16[128,1024]{1,0:T(8,128)(2,1)}, bf16[128,1024]{1,0:T(8,128)(2,1)}, u32[]{:S(2)}, u32[]{:S(2)}) collective-permute-start(bf16[128,1024]{1,0:T(8,128)(2,1)} %bitcast.15), channel_id=1, source_target_pairs={{0,8},{2,10},{4,12},{6,14},{8,0},{10,2},{12,4},{14,6},{16,24},{18,... | collective-permute-start | bytes 786440 | tf_op jit(solution)/shard_map/ppermute | solution.py:16
  36.4 19.1 %collective-permute-start.5 = (bf16[128,1024]{1,0:T(8,128)(2,1)}, bf16[128,1024]{1,0:T(8,128)(2,1)}, u32[]{:S(2)}, u32[]{:S(2)}) collective-permute-start(bf16[128,1024]{1,0:T(8,128)(2,1)} %bitcast.15), channel_id=1, source_target_pairs={{0,4},{2,6},{4,0},{6,2},{8,12},{10,14},{12,8},{14,10},{16,20},{18,... | collective-permute-start | bytes 786440 | tf_op jit(solution)/shard_map/ppermute | solution.py:16
  37.6 22.0 %collective-permute-start.1 = (bf16[128,1024]{1,0:T(8,128)(2,1)}, bf16[128,1024]{1,0:T(8,128)(2,1)}, u32[]{:S(2)}, u32[]{:S(2)}) collective-permute-start(bf16[128,1024]{1,0:T(8,128)(2,1)} %bitcast.15), channel_id=1, source_target_pairs={{0,2},{2,0},{4,6},{6,4},{8,10},{10,8},{12,14},{14,12},{16,18},{18,... | collective-permute-start | bytes 786440 | tf_op jit(solution)/shard_map/ppermute | solution.py:16
  37.6 28.4 %collective-permute-start.15 = (bf16[128,1024]{1,0:T(8,128)(2,1)}, bf16[128,1024]{1,0:T(8,128)(2,1)}, u32[]{:S(2)}, u32[]{:S(2)}) collective-permute-start(bf16[128,1024]{1,0:T(8,128)(2,1)} %bitcast.22), channel_id=1, source_target_pairs={{0,16},{2,18},{4,20},{6,22},{8,24},{10,26},{12,28},{14,30},{16,0},... | collective-permute-start | bytes 786440 | tf_op jit(solution)/shard_map/ppermute | solution.py:16
  47.8 22.0 %collective-permute-start.11 = (bf16[128,1024]{1,0:T(8,128)(2,1)}, bf16[128,1024]{1,0:T(8,128)(2,1)}, u32[]{:S(2)}, u32[]{:S(2)}) collective-permute-start(bf16[128,1024]{1,0:T(8,128)(2,1)} %bitcast.22), channel_id=1, source_target_pairs={{0,8},{2,10},{4,12},{6,14},{8,0},{10,2},{12,4},{14,6},{16,24},{18,... | collective-permute-start | bytes 786440 | tf_op jit(solution)/shard_map/ppermute | solution.py:16
  50.2 23.9 %collective-permute-start.7 = (bf16[128,1024]{1,0:T(8,128)(2,1)}, bf16[128,1024]{1,0:T(8,128)(2,1)}, u32[]{:S(2)}, u32[]{:S(2)}) collective-permute-start(bf16[128,1024]{1,0:T(8,128)(2,1)} %bitcast.22), channel_id=1, source_target_pairs={{0,4},{2,6},{4,0},{6,2},{8,12},{10,14},{12,8},{14,10},{16,20},{18,... | collective-permute-start | bytes 786440 | tf_op jit(solution)/shard_map/ppermute | solution.py:16
  55.5 22.8 %collective-permute-start.3 = (bf16[128,1024]{1,0:T(8,128)(2,1)}, bf16[128,1024]{1,0:T(8,128)(2,1)}, u32[]{:S(2)}, u32[]{:S(2)}) collective-permute-start(bf16[128,1024]{1,0:T(8,128)(2,1)} %bitcast.22), channel_id=1, source_target_pairs={{0,2},{2,0},{4,6},{6,4},{8,10},{10,8},{12,14},{14,12},{16,18},{18,... | collective-permute-start | bytes 786440 | tf_op jit(solution)/shard_map/ppermute | solution.py:16
  105.1 8.7 %copy-start.30 = (f32[64]{0:T(128)S(1)}, f32[64]{0:T(128)}, u32[]{:S(2)}) copy-start(f32[64]{0:T(128)} %get-tuple-element.69) | copy-start | bytes 772
  105.1 8.7 %copy-start.31 = (f32[64]{0:T(128)S(1)}, f32[64]{0:T(128)}, u32[]{:S(2)}) copy-start(f32[64]{0:T(128)} %get-tuple-element.70) | copy-start | bytes 772
  105.1 8.7 %copy-start.32 = (f32[64]{0:T(128)S(1)}, f32[64]{0:T(128)}, u32[]{:S(2)}) copy-start(f32[64]{0:T(128)} %get-tuple-element.71) | copy-start | bytes 772
  106.1 9.3 %copy-start.7 = (f32[16,128,128]{1,2,0:T(8,128)S(1)}, f32[16,128,128]{1,2,0:T(8,128)}, u32[]{:S(2)}) copy-start(f32[16,128,128]{1,2,0:T(8,128)} %copy-done.5) | copy-start | bytes 3145732
  108.0 16.1 %collective-permute-start.19 = (bf16[128,1024]{0,1:T(8,128)(2,1)}, bf16[128,1024]{0,1:T(8,128)(2,1)}, u32[]{:S(2)}, u32[]{:S(2)}) collective-permute-start(bf16[128,1024]{0,1:T(8,128)(2,1)} %bitcast.353), channel_id=1, source_target_pairs={{0,16},{2,18},{4,20},{6,22},{8,24},{10,26},{12,28},{14,30},{16,0},... | collective-permute-start | bytes 786440 | tf_op jit(solution)/shard_map/ppermute | solution.py:16
  110.9 13.7 %collective-permute-start.18 = (bf16[128,1024]{0,1:T(8,128)(2,1)}, bf16[128,1024]{0,1:T(8,128)(2,1)}, u32[]{:S(2)}, u32[]{:S(2)}) collective-permute-start(bf16[128,1024]{0,1:T(8,128)(2,1)} %bitcast.352), channel_id=1, source_target_pairs={{0,8},{2,10},{4,12},{6,14},{8,0},{10,2},{12,4},{14,6},{16,24},{18,... | collective-permute-start | bytes 786440 | tf_op jit(solution)/shard_map/ppermute | solution.py:16
  110.9 15.0 %collective-permute-start.17 = (bf16[128,1024]{0,1:T(8,128)(2,1)}, bf16[128,1024]{0,1:T(8,128)(2,1)}, u32[]{:S(2)}, u32[]{:S(2)}) collective-permute-start(bf16[128,1024]{0,1:T(8,128)(2,1)} %bitcast.355), channel_id=1, source_target_pairs={{0,4},{2,6},{4,0},{6,2},{8,12},{10,14},{12,8},{14,10},{16,20},{18,... | collective-permute-start | bytes 786440 | tf_op jit(solution)/shard_map/ppermute | solution.py:16
  111.7 14.1 %collective-permute-start.16 = (bf16[128,1024]{0,1:T(8,128)(2,1)}, bf16[128,1024]{0,1:T(8,128)(2,1)}, u32[]{:S(2)}, u32[]{:S(2)}) collective-permute-start(bf16[128,1024]{0,1:T(8,128)(2,1)} %bitcast.354), channel_id=1, source_target_pairs={{0,2},{2,0},{4,6},{6,4},{8,10},{10,8},{12,14},{14,12},{16,18},{18,... | collective-permute-start | bytes 786440 | tf_op jit(solution)/shard_map/ppermute | solution.py:16
  111.7 24.5 %collective-permute-start.23 = (bf16[128,1024]{0,1:T(8,128)(2,1)}, bf16[128,1024]{0,1:T(8,128)(2,1)S(1)}, u32[]{:S(2)}, u32[]{:S(2)}) collective-permute-start(bf16[128,1024]{0,1:T(8,128)(2,1)} %bitcast.343), channel_id=1, source_target_pairs={{0,16},{2,18},{4,20},{6,22},{8,24},{10,26},{12,28},{14,30},{16,0},... | collective-permute-start | bytes 786440 | tf_op jit(solution)/shard_map/ppermute | solution.py:16
  115.4 8.7 %copy-start.21 = (bf16[16,128,64]{1,2,0:T(8,128)(2,1)S(1)}, bf16[16,128,64]{1,2,0:T(8,128)(2,1)}, u32[]{:S(2)}) copy-start(bf16[16,128,64]{1,2,0:T(8,128)(2,1)} %convolution_convert_fusion.1) | copy-start | bytes 786436
  115.4 9.2 %copy-start.20 = (bf16[16,128,64]{1,2,0:T(8,128)(2,1)S(1)}, bf16[16,128,64]{1,2,0:T(8,128)(2,1)}, u32[]{:S(2)}) copy-start(bf16[16,128,64]{1,2,0:T(8,128)(2,1)} %convolution_convert_fusion.2) | copy-start | bytes 786436
  124.1 13.2 %collective-permute-start.22 = (bf16[128,1024]{0,1:T(8,128)(2,1)S(1)}, bf16[128,1024]{0,1:T(8,128)(2,1)S(1)}, u32[]{:S(2)}, u32[]{:S(2)}) collective-permute-start(bf16[128,1024]{0,1:T(8,128)(2,1)S(1)} %bitcast.342), channel_id=1, source_target_pairs={{0,8},{2,10},{4,12},{6,14},{8,0},{10,2},{12,4},{14,6},{16,24},{18,... | collective-permute-start | bytes 786440 | tf_op jit(solution)/shard_map/ppermute | solution.py:16
  124.6 12.7 %collective-permute-start.21 = (bf16[128,1024]{0,1:T(8,128)(2,1)S(1)}, bf16[128,1024]{0,1:T(8,128)(2,1)S(1)}, u32[]{:S(2)}, u32[]{:S(2)}) collective-permute-start(bf16[128,1024]{0,1:T(8,128)(2,1)S(1)} %bitcast.341), channel_id=1, source_target_pairs={{0,4},{2,6},{4,0},{6,2},{8,12},{10,14},{12,8},{14,10},{16,20},{18,... | collective-permute-start | bytes 786440 | tf_op jit(solution)/shard_map/ppermute | solution.py:16
  125.8 11.5 %collective-permute-start.20 = (bf16[128,1024]{0,1:T(8,128)(2,1)S(1)}, bf16[128,1024]{0,1:T(8,128)(2,1)S(1)}, u32[]{:S(2)}, u32[]{:S(2)}) collective-permute-start(bf16[128,1024]{0,1:T(8,128)(2,1)S(1)} %bitcast.345), channel_id=1, source_target_pairs={{0,2},{2,0},{4,6},{6,4},{8,10},{10,8},{12,14},{14,12},{16,18},{18,... | collective-permute-start | bytes 786440 | tf_op jit(solution)/shard_map/ppermute | solution.py:16
  (27 other events, 52.6 us)
Sparse Core Ops, SparseCore 0:
  115.5 132.5 all-reduce.1
where the time goes:
time: 258 us; the launch traced here: 257 us
  waiting for transfers between devices  136 us (53%)
  matrix products  38.1 us (15%)
  local copies, waits for them, and re-layouts  28.9 us (11%)
  starting transfers between devices  26.2 us (10%)
  between operations  17.7 us (7%)
  other arithmetic  9.98 us (4%)
    psum x1, waiting for transfers between devices, local(): table_total = lax.psum(table_acc, ('seq', 'dp'))  109 us
    ppermute x24, waiting for transfers between devices, from_partner(): return lax.ppermute(value, axis, pairs)  27.1 us
    ppermute x24, starting transfers between devices, from_partner(): return lax.ppermute(value, axis, pairs)  26.2 us
    unnamed x77, local copies, waits for them, and re-layouts  14.8 us
    ppermute x8, local copies, waits for them, and re-layouts, from_partner(): return lax.ppermute(value, axis, pairs)  13.4 us
    dot_general x5, matrix products, local(): jnp.einsum('htu,uhd->thd', weights.astype(jnp.bfloat16), value_heads, pre...  11 us
    dot_general x5, matrix products, masked_scores(): jnp.einsum('thd,uhd->htu', query_heads, key_heads, preferred_element_type...  7.82 us
  transfers between devices with their start and end apart: 25, of which 9 were waited for; matrix products, arithmetic and copies ran while one was open for 17% of the time, Pallas kernels for 0%

commit v1 on v0

--- a/solution.py
+++ b/solution.py
@@ -169,7 +169,8 @@
             )
             key_acc = key_acc + back_keys.reshape(row_count, H, DH).astype(jnp.float32)
             value_acc = value_acc + back_values.reshape(row_count, H, DH).astype(jnp.float32)
-    table_total = lax.psum(table_acc, ("seq", "dp"))
+    partial = lax.psum(table_acc, "dp")
+    table_total = lax.psum(partial, "seq")
     feature_count = H * DH
     return (
         out_rows.reshape(1, row_count, feature_count),

time: 258 us -> 247 us (0.957)
  waiting for transfers between devices: 136 us -> 122 us
    ppermute x24, waiting for transfers between devices: 27.1 us -> 13.2 us  [from_partner(): return lax.ppermute(value, axis, pairs)]
    psum x1 -> x2, waiting for transfers between devices: 109 us -> 109 us  [the longest x1 81.8 us: local(): table_total = lax.psum(partial, 'seq')]
  transfers between devices with their start and end apart: 25 -> 26, of which waited for: 9 -> 8; matrix products, arithmetic and copies ran while one was open for 17% -> 18% of each run, Pallas kernels for 0% -> 0%
where the time goes in v1:
time: 247 us; the launch traced here: 246 us
  waiting for transfers between devices  122 us (49%)
  matrix products  38.8 us (16%)
  local copies, waits for them, and re-layouts  29.8 us (12%)
  starting transfers between devices  28 us (11%)
  between operations  17.7 us (7%)
  other arithmetic  9.97 us (4%)
    psum x1, waiting for transfers between devices, local(): table_total = lax.psum(partial, 'seq')  81.8 us
    ppermute x24, starting transfers between devices, from_partner(): return lax.ppermute(value, axis, pairs)  27.9 us
    psum x1, waiting for transfers between devices, local(): partial = lax.psum(table_acc, 'dp')  27.3 us
    unnamed x77, local copies, waits for them, and re-layouts  15.7 us
    ppermute x8, local copies, waits for them, and re-layouts, from_partner(): return lax.ppermute(value, axis, pairs)  13.4 us
    ppermute x24, waiting for transfers between devices, from_partner(): return lax.ppermute(value, axis, pairs)  13.2 us
    dot_general x5, matrix products, local(): jnp.einsum('htu,uhd->thd', weights.astype(jnp.bfloat16), value_heads, pre...  11 us
    dot_general x5, matrix products, masked_scores(): jnp.einsum('thd,uhd->htu', query_heads, key_heads, preferred_element_type...  7.82 us
  transfers between devices with their start and end apart: 26, of which 8 were waited for; matrix products, arithmetic and copies ran while one was open for 18% of the time, Pallas kernels for 0%

profile of v1, /device:TPU:0, one launch (start us, length us, event | category | flops | bytes accessed | tf_op | source)
XLA Modules:
  0.0 246.4 jit_solution(10164629875464693465)
XLA Ops:
  8.0 3.0 %collective-permute-start.4 = (bf16[128]{0:T(256)(128)(2,1)S(1)}, bf16[128]{0:T(256)(128)(2,1)S(1)}, u32[]{:S(2)}, u32[]{:S(2)}) collective-permute-start(bf16[128]{0:T(256)(128)(2,1)S(1)} %get-tuple-element.40), channel_id=1, source_target_pairs={{0,4},{2,6},{4,0},{6,2},{8,12},{10,14},{12,8},{14,10},{16,20},{18,... | collective-permute-start | bytes 776 | tf_op jit(solution)/shard_map/ppermute | solution.py:16
  10.9 1.6 collective-permute-start.8
  12.5 2.6 %collective-permute-start.12 = (bf16[128]{0:T(256)(128)(2,1)S(1)}, bf16[128]{0:T(256)(128)(2,1)S(1)}, u32[]{:S(2)}, u32[]{:S(2)}) collective-permute-start(bf16[128]{0:T(256)(128)(2,1)S(1)} %get-tuple-element.40), channel_id=1, source_target_pairs={{0,16},{2,18},{4,20},{6,22},{8,24},{10,26},{12,28},{14,30},{16,0},... | collective-permute-start | bytes 776 | tf_op jit(solution)/shard_map/ppermute | solution.py:16
  15.8 1.7 collective-permute-start.14
  23.2 1.8 collective-permute-start.10
  26.7 1.8 collective-permute-start.6
  31.8 2.6 %collective-permute-start.13 = (bf16[128,1024]{1,0:T(8,128)(2,1)}, bf16[128,1024]{1,0:T(8,128)(2,1)S(1)}, u32[]{:S(2)}, u32[]{:S(2)}) collective-permute-start(bf16[128,1024]{1,0:T(8,128)(2,1)} %bitcast.15), channel_id=1, source_target_pairs={{0,16},{2,18},{4,20},{6,22},{8,24},{10,26},{12,28},{14,30},{16,0},... | collective-permute-start | bytes 786440 | tf_op jit(solution)/shard_map/ppermute | solution.py:16
  38.0 2.6 %broadcast_compare_fusion = (pred[128,128]{0,1:T(8,128)(4,1)S(1)}, pred[128,128]{0,1:T(8,128)(4,1)S(1)}, pred[128,128]{0,1:T(8,128)(4,1)S(1)}, pred[128,128]{0,1:T(8,128)(4,1)S(1)}, pred[128,128]{0,1:T(8,128)(4,1)S(1)}) fusion(f32[128]{0:T(128)S(1)} %get-tuple-element.41, pred[]{:T(512)} %bitcast.25, f32[128]{0:T(128)S(1)} %convert_element_type.245, ...), kind=kLoop, calls=%fused_computation.151 | loop fusion | flops 147456 | bytes 84484 | tf_op jit(solution)/shard_map/eq | solution.py:43
  41.1 6.8 %collective-permute-done.13 = bf16[128,1024]{1,0:T(8,128)(2,1)S(1)} collective-permute-done((bf16[128,1024]{1,0:T(8,128)(2,1)}, bf16[128,1024]{1,0:T(8,128)(2,1)S(1)}, u32[]{:S(2)}, u32[]{:S(2)}) %collective-permute-start.13) | collective-permute-done | bytes 262176 | tf_op jit(solution)/shard_map/ppermute | solution.py:16
  51.4 1.8 copy.75
  53.2 2.3 fusion.151
  55.5 1.8 copy.72
  57.3 2.3 fusion.152
  59.6 1.8 copy.69
  66.0 1.8 copy.79
  67.8 2.0 convolution_bitcast_fusion
  69.9 1.8 copy.76
  71.7 2.4 convolution_bitcast_fusion.1
  74.1 1.8 copy.73
  75.8 2.4 convolution_bitcast_fusion.2
  78.3 1.8 copy.70
  80.8 3.1 %multiply_reduce_fusion = (f32[128,16]{0,1:T(8,128)S(1)}, bf16[128,16,64]{0,2,1:T(8,128)(2,1)}) fusion(bf16[128,16,64]{0,2,1:T(8,128)(2,1)S(1)} %bitcast.299, f32[128,16]{0,1:T(8,128)S(1)} %copy-done.24, f32[128,16,64]{0,2,1:T(8,128)} %convolution_bitcast_fusion, f32[128,16]{0,1:T(8,128)S(1)} %copy-done.27, f32[128,16,64]{0,2,1:T(8,128)} %convolution_bitcast_fusion.1, ...), kind=kOutput, calls=%fused_computation.103 | convolution fusion | flops 36042752 | bytes 3997696 | tf_op jit(solution)/shard_map/htu,uhd->thd/dot_general | solution.py:112
  99.8 1.9 copy.102
  106.1 1.9 copy.103
  108.0 2.9 %collective-permute-start.19 = (bf16[128,1024]{0,1:T(8,128)(2,1)}, bf16[128,1024]{0,1:T(8,128)(2,1)}, u32[]{:S(2)}, u32[]{:S(2)}) collective-permute-start(bf16[128,1024]{0,1:T(8,128)(2,1)} %bitcast.353), channel_id=1, source_target_pairs={{0,16},{2,18},{4,20},{6,22},{8,24},{10,26},{12,28},{14,30},{16,0},... | collective-permute-start | bytes 786440 | tf_op jit(solution)/shard_map/ppermute | solution.py:16
  111.7 2.0 collective-permute-start.23
  113.8 1.5 multiply_add_fusion
  116.6 27.3 %all-reduce.3.cloned.1.call-done = f32[16,64,64]{2,1,0:T(8,128)} async-done(((f32[16,64,64]{2,1,0:T(8,128)}), f32[16,64,64]{2,1,0:T(8,128)}) %all-reduce.3.cloned.1.call-update) | async-done | bytes 262160 | tf_op jit(solution)/shard_map/psum | solution.py:172
  144.8 1.5 collective-permute-start.22
  149.2 3.7 %collective-permute-done.22 = bf16[128,1024]{0,1:T(8,128)(2,1)S(1)} collective-permute-done((bf16[128,1024]{0,1:T(8,128)(2,1)S(1)}, bf16[128,1024]{0,1:T(8,128)(2,1)S(1)}, u32[]{:S(2)}, u32[]{:S(2)}) %collective-permute-start.22) | collective-permute-done | bytes 262176 | tf_op jit(solution)/shard_map/ppermute | solution.py:16
  156.0 81.8 %all-reduce.5.cloned.1.call-done = f32[16,64,64]{2,1,0:T(8,128)} async-done(((f32[16,64,64]{2,1,0:T(8,128)}), f32[16,64,64]{2,1,0:T(8,128)}) %all-reduce.5.cloned.1.call-update) | async-done | bytes 262160 | tf_op jit(solution)/shard_map/psum | solution.py:173
  237.7 1.9 copy.135
  (165 shorter events, 51.1 us)
Async XLA Ops:
  7.2 12.0 %copy-start = (bf16[16,64,64]{2,1,0:T(8,128)(2,1)S(1)}, bf16[16,64,64]{2,1,0:T(8,128)(2,1)}, u32[]{:S(2)}) copy-start(bf16[16,64,64]{2,1,0:T(8,128)(2,1)} %param.15) | copy-start | bytes 393220
  7.2 136.7 %all-reduce.3.cloned.1.call-start = ((), (), s32[]{:S(2)}) async-start(), calls=%async_computation | async-start | bytes 1048576 | tf_op jit(solution)/shard_map/psum | solution.py:172
  8.0 27.9 %collective-permute-start.4 = (bf16[128]{0:T(256)(128)(2,1)S(1)}, bf16[128]{0:T(256)(128)(2,1)S(1)}, u32[]{:S(2)}, u32[]{:S(2)}) collective-permute-start(bf16[128]{0:T(256)(128)(2,1)S(1)} %get-tuple-element.40), channel_id=1, source_target_pairs={{0,4},{2,6},{4,0},{6,2},{8,12},{10,14},{12,8},{14,10},{16,20},{18,... | collective-permute-start | bytes 776 | tf_op jit(solution)/shard_map/ppermute | solution.py:16
  10.9 25.5 %collective-permute-start.8 = (bf16[128]{0:T(256)(128)(2,1)S(1)}, bf16[128]{0:T(256)(128)(2,1)S(1)}, u32[]{:S(2)}, u32[]{:S(2)}) collective-permute-start(bf16[128]{0:T(256)(128)(2,1)S(1)} %get-tuple-element.40), channel_id=1, source_target_pairs={{0,8},{2,10},{4,12},{6,14},{8,0},{10,2},{12,4},{14,6},{16,24},{18,... | collective-permute-start | bytes 776 | tf_op jit(solution)/shard_map/ppermute | solution.py:16
  12.5 25.1 %collective-permute-start.12 = (bf16[128]{0:T(256)(128)(2,1)S(1)}, bf16[128]{0:T(256)(128)(2,1)S(1)}, u32[]{:S(2)}, u32[]{:S(2)}) collective-permute-start(bf16[128]{0:T(256)(128)(2,1)S(1)} %get-tuple-element.40), channel_id=1, source_target_pairs={{0,16},{2,18},{4,20},{6,22},{8,24},{10,26},{12,28},{14,30},{16,0},... | collective-permute-start | bytes 776 | tf_op jit(solution)/shard_map/ppermute | solution.py:16
  15.1 22.5 %collective-permute-start = (bf16[128]{0:T(256)(128)(2,1)S(1)}, bf16[128]{0:T(256)(128)(2,1)S(1)}, u32[]{:S(2)}, u32[]{:S(2)}) collective-permute-start(bf16[128]{0:T(256)(128)(2,1)S(1)} %get-tuple-element.40), channel_id=1, source_target_pairs={{0,2},{2,0},{4,6},{6,4},{8,10},{10,8},{12,14},{14,12},{16,18},{18,... | collective-permute-start | bytes 776 | tf_op jit(solution)/shard_map/ppermute | solution.py:16
  15.8 7.4 %collective-permute-start.14 = (bf16[1]{0:T(256)(128)(2,1)}, bf16[1]{0:T(256)(128)(2,1)}, u32[]{:S(2)}, u32[]{:S(2)}) collective-permute-start(bf16[1]{0:T(256)(128)(2,1)} %bitcast.17), channel_id=1, source_target_pairs={{0,16},{2,18},{4,20},{6,22},{8,24},{10,26},{12,28},{14,30},{16,0},... | collective-permute-start | bytes 14 | tf_op jit(solution)/shard_map/ppermute | solution.py:16
  23.2 3.6 %collective-permute-start.10 = (bf16[1]{0:T(256)(128)(2,1)}, bf16[1]{0:T(256)(128)(2,1)}, u32[]{:S(2)}, u32[]{:S(2)}) collective-permute-start(bf16[1]{0:T(256)(128)(2,1)} %bitcast.17), channel_id=1, source_target_pairs={{0,8},{2,10},{4,12},{6,14},{8,0},{10,2},{12,4},{14,6},{16,24},{18,... | collective-permute-start | bytes 14 | tf_op jit(solution)/shard_map/ppermute | solution.py:16
  26.7 3.5 %collective-permute-start.6 = (bf16[1]{0:T(256)(128)(2,1)}, bf16[1]{0:T(256)(128)(2,1)}, u32[]{:S(2)}, u32[]{:S(2)}) collective-permute-start(bf16[1]{0:T(256)(128)(2,1)} %bitcast.17), channel_id=1, source_target_pairs={{0,4},{2,6},{4,0},{6,2},{8,12},{10,14},{12,8},{14,10},{16,20},{18,... | collective-permute-start | bytes 14 | tf_op jit(solution)/shard_map/ppermute | solution.py:16
  30.2 1.6 collective-permute-start.2
  31.8 16.0 %collective-permute-start.13 = (bf16[128,1024]{1,0:T(8,128)(2,1)}, bf16[128,1024]{1,0:T(8,128)(2,1)S(1)}, u32[]{:S(2)}, u32[]{:S(2)}) collective-permute-start(bf16[128,1024]{1,0:T(8,128)(2,1)} %bitcast.15), channel_id=1, source_target_pairs={{0,16},{2,18},{4,20},{6,22},{8,24},{10,26},{12,28},{14,30},{16,0},... | collective-permute-start | bytes 786440 | tf_op jit(solution)/shard_map/ppermute | solution.py:16
  35.8 14.4 %collective-permute-start.9 = (bf16[128,1024]{1,0:T(8,128)(2,1)}, bf16[128,1024]{1,0:T(8,128)(2,1)}, u32[]{:S(2)}, u32[]{:S(2)}) collective-permute-start(bf16[128,1024]{1,0:T(8,128)(2,1)} %bitcast.15), channel_id=1, source_target_pairs={{0,8},{2,10},{4,12},{6,14},{8,0},{10,2},{12,4},{14,6},{16,24},{18,... | collective-permute-start | bytes 786440 | tf_op jit(solution)/shard_map/ppermute | solution.py:16
  36.4 19.1 %collective-permute-start.5 = (bf16[128,1024]{1,0:T(8,128)(2,1)}, bf16[128,1024]{1,0:T(8,128)(2,1)}, u32[]{:S(2)}, u32[]{:S(2)}) collective-permute-start(bf16[128,1024]{1,0:T(8,128)(2,1)} %bitcast.15), channel_id=1, source_target_pairs={{0,4},{2,6},{4,0},{6,2},{8,12},{10,14},{12,8},{14,10},{16,20},{18,... | collective-permute-start | bytes 786440 | tf_op jit(solution)/shard_map/ppermute | solution.py:16
  37.6 22.0 %collective-permute-start.1 = (bf16[128,1024]{1,0:T(8,128)(2,1)}, bf16[128,1024]{1,0:T(8,128)(2,1)}, u32[]{:S(2)}, u32[]{:S(2)}) collective-permute-start(bf16[128,1024]{1,0:T(8,128)(2,1)} %bitcast.15), channel_id=1, source_target_pairs={{0,2},{2,0},{4,6},{6,4},{8,10},{10,8},{12,14},{14,12},{16,18},{18,... | collective-permute-start | bytes 786440 | tf_op jit(solution)/shard_map/ppermute | solution.py:16
  37.6 28.4 %collective-permute-start.15 = (bf16[128,1024]{1,0:T(8,128)(2,1)}, bf16[128,1024]{1,0:T(8,128)(2,1)}, u32[]{:S(2)}, u32[]{:S(2)}) collective-permute-start(bf16[128,1024]{1,0:T(8,128)(2,1)} %bitcast.22), channel_id=1, source_target_pairs={{0,16},{2,18},{4,20},{6,22},{8,24},{10,26},{12,28},{14,30},{16,0},... | collective-permute-start | bytes 786440 | tf_op jit(solution)/shard_map/ppermute | solution.py:16
  47.8 22.0 %collective-permute-start.11 = (bf16[128,1024]{1,0:T(8,128)(2,1)}, bf16[128,1024]{1,0:T(8,128)(2,1)}, u32[]{:S(2)}, u32[]{:S(2)}) collective-permute-start(bf16[128,1024]{1,0:T(8,128)(2,1)} %bitcast.22), channel_id=1, source_target_pairs={{0,8},{2,10},{4,12},{6,14},{8,0},{10,2},{12,4},{14,6},{16,24},{18,... | collective-permute-start | bytes 786440 | tf_op jit(solution)/shard_map/ppermute | solution.py:16
  50.2 23.9 %collective-permute-start.7 = (bf16[128,1024]{1,0:T(8,128)(2,1)}, bf16[128,1024]{1,0:T(8,128)(2,1)}, u32[]{:S(2)}, u32[]{:S(2)}) collective-permute-start(bf16[128,1024]{1,0:T(8,128)(2,1)} %bitcast.22), channel_id=1, source_target_pairs={{0,4},{2,6},{4,0},{6,2},{8,12},{10,14},{12,8},{14,10},{16,20},{18,... | collective-permute-start | bytes 786440 | tf_op jit(solution)/shard_map/ppermute | solution.py:16
  55.5 22.8 %collective-permute-start.3 = (bf16[128,1024]{1,0:T(8,128)(2,1)}, bf16[128,1024]{1,0:T(8,128)(2,1)}, u32[]{:S(2)}, u32[]{:S(2)}) collective-permute-start(bf16[128,1024]{1,0:T(8,128)(2,1)} %bitcast.22), channel_id=1, source_target_pairs={{0,2},{2,0},{4,6},{6,4},{8,10},{10,8},{12,14},{14,12},{16,18},{18,... | collective-permute-start | bytes 786440 | tf_op jit(solution)/shard_map/ppermute | solution.py:16
  105.1 8.7 %copy-start.29 = (f32[64]{0:T(128)S(1)}, f32[64]{0:T(128)}, u32[]{:S(2)}) copy-start(f32[64]{0:T(128)} %get-tuple-element.68) | copy-start | bytes 772
  105.1 8.7 %copy-start.30 = (f32[64]{0:T(128)S(1)}, f32[64]{0:T(128)}, u32[]{:S(2)}) copy-start(f32[64]{0:T(128)} %get-tuple-element.69) | copy-start | bytes 772
  105.1 8.7 %copy-start.31 = (f32[64]{0:T(128)S(1)}, f32[64]{0:T(128)}, u32[]{:S(2)}) copy-start(f32[64]{0:T(128)} %get-tuple-element.70) | copy-start | bytes 772
  105.1 8.7 %copy-start.32 = (f32[64]{0:T(128)S(1)}, f32[64]{0:T(128)}, u32[]{:S(2)}) copy-start(f32[64]{0:T(128)} %get-tuple-element.71) | copy-start | bytes 772
  106.1 9.3 %copy-start.7 = (f32[16,128,128]{1,2,0:T(8,128)S(1)}, f32[16,128,128]{1,2,0:T(8,128)}, u32[]{:S(2)}) copy-start(f32[16,128,128]{1,2,0:T(8,128)} %copy-done.5) | copy-start | bytes 3145732
  108.0 35.9 %collective-permute-start.19 = (bf16[128,1024]{0,1:T(8,128)(2,1)}, bf16[128,1024]{0,1:T(8,128)(2,1)}, u32[]{:S(2)}, u32[]{:S(2)}) collective-permute-start(bf16[128,1024]{0,1:T(8,128)(2,1)} %bitcast.353), channel_id=1, source_target_pairs={{0,16},{2,18},{4,20},{6,22},{8,24},{10,26},{12,28},{14,30},{16,0},... | collective-permute-start | bytes 786440 | tf_op jit(solution)/shard_map/ppermute | solution.py:16
  110.9 35.4 %collective-permute-start.18 = (bf16[128,1024]{0,1:T(8,128)(2,1)}, bf16[128,1024]{0,1:T(8,128)(2,1)}, u32[]{:S(2)}, u32[]{:S(2)}) collective-permute-start(bf16[128,1024]{0,1:T(8,128)(2,1)} %bitcast.352), channel_id=1, source_target_pairs={{0,8},{2,10},{4,12},{6,14},{8,0},{10,2},{12,4},{14,6},{16,24},{18,... | collective-permute-start | bytes 786440 | tf_op jit(solution)/shard_map/ppermute | solution.py:16
  110.9 36.9 %collective-permute-start.17 = (bf16[128,1024]{0,1:T(8,128)(2,1)}, bf16[128,1024]{0,1:T(8,128)(2,1)}, u32[]{:S(2)}, u32[]{:S(2)}) collective-permute-start(bf16[128,1024]{0,1:T(8,128)(2,1)} %bitcast.355), channel_id=1, source_target_pairs={{0,4},{2,6},{4,0},{6,2},{8,12},{10,14},{12,8},{14,10},{16,20},{18,... | collective-permute-start | bytes 786440 | tf_op jit(solution)/shard_map/ppermute | solution.py:16
  111.7 36.1 %collective-permute-start.16 = (bf16[128,1024]{0,1:T(8,128)(2,1)}, bf16[128,1024]{0,1:T(8,128)(2,1)}, u32[]{:S(2)}, u32[]{:S(2)}) collective-permute-start(bf16[128,1024]{0,1:T(8,128)(2,1)} %bitcast.354), channel_id=1, source_target_pairs={{0,2},{2,0},{4,6},{6,4},{8,10},{10,8},{12,14},{14,12},{16,18},{18,... | collective-permute-start | bytes 786440 | tf_op jit(solution)/shard_map/ppermute | solution.py:16
  111.7 37.5 %collective-permute-start.23 = (bf16[128,1024]{0,1:T(8,128)(2,1)}, bf16[128,1024]{0,1:T(8,128)(2,1)S(1)}, u32[]{:S(2)}, u32[]{:S(2)}) collective-permute-start(bf16[128,1024]{0,1:T(8,128)(2,1)} %bitcast.343), channel_id=1, source_target_pairs={{0,16},{2,18},{4,20},{6,22},{8,24},{10,26},{12,28},{14,30},{16,0},... | collective-permute-start | bytes 786440 | tf_op jit(solution)/shard_map/ppermute | solution.py:16
  115.4 122.4 %all-reduce.5.cloned.1.call-start = ((), (), s32[]{:S(2)}) async-start(), calls=%async_computation.1 | async-start | bytes 1048576 | tf_op jit(solution)/shard_map/psum | solution.py:173
  144.8 8.0 %collective-permute-start.22 = (bf16[128,1024]{0,1:T(8,128)(2,1)S(1)}, bf16[128,1024]{0,1:T(8,128)(2,1)S(1)}, u32[]{:S(2)}, u32[]{:S(2)}) collective-permute-start(bf16[128,1024]{0,1:T(8,128)(2,1)S(1)} %bitcast.342), channel_id=1, source_target_pairs={{0,8},{2,10},{4,12},{6,14},{8,0},{10,2},{12,4},{14,6},{16,24},{18,... | collective-permute-start | bytes 786440 | tf_op jit(solution)/shard_map/ppermute | solution.py:16
  146.3 7.8 %collective-permute-start.21 = (bf16[128,1024]{0,1:T(8,128)(2,1)S(1)}, bf16[128,1024]{0,1:T(8,128)(2,1)S(1)}, u32[]{:S(2)}, u32[]{:S(2)}) collective-permute-start(bf16[128,1024]{0,1:T(8,128)(2,1)S(1)} %bitcast.341), channel_id=1, source_target_pairs={{0,4},{2,6},{4,0},{6,2},{8,12},{10,14},{12,8},{14,10},{16,20},{18,... | collective-permute-start | bytes 786440 | tf_op jit(solution)/shard_map/ppermute | solution.py:16
  147.8 6.3 %collective-permute-start.20 = (bf16[128,1024]{0,1:T(8,128)(2,1)}, bf16[128,1024]{0,1:T(8,128)(2,1)S(1)}, u32[]{:S(2)}, u32[]{:S(2)}) collective-permute-start(bf16[128,1024]{0,1:T(8,128)(2,1)} %bitcast.345), channel_id=1, source_target_pairs={{0,2},{2,0},{4,6},{6,4},{8,10},{10,8},{12,14},{14,12},{16,18},{18,... | collective-permute-start | bytes 786440 | tf_op jit(solution)/shard_map/ppermute | solution.py:16
  (28 other events, 47.3 us)
Sparse Core Ops, SparseCore 0:
  115.5 28.3 all-reduce.2
  147.6 90.0 all-reduce.4
